TPU v7x, 256 devices: a whole 4x4x8 slice. The times are simulated.
256 devices in a mesh: date: 16 (over x, y_hi, core), rng: 16 (over z, y_lo).
Axes of the slice: x: 4, y: 4 (y_hi: 2, y_lo: 2; y = y_hi * 2 + y_lo), z: 8, core: 2. Of those that a mesh axis runs over, the one named last changes fastest.
Arguments:
- slave_complex_pixels: bfloat16 [32, 2, 128, 4096], P(None, None, 'date', 'rng')
- along_track_line_groups: int32 [32, 16, 64], P(None, 'rng'), may hold values from 0 to 126, as said below
- master_epoch_position: int32 [1], replicated, may hold values from 0 to 31
- sweep_identifier: int32 [64], replicated, may hold values from 0 to 1, never falling along the last dimension, each value on 1 to 48 neighbouring positions
- initial_filter_kernel: float32 [32, 5, 3, 3], replicated, may hold values from -0.875 to 0.875
- initial_filter_shift: float32 [32], replicated, may hold values from -3 to 3
- latter_filter_kernel: float32 [2, 32, 3, 3], replicated, may hold values from -0.375 to 0.375
- latter_filter_shift: float32 [2], replicated, may hold values from -3 to 3
Outputs:
- burn_logits: float32 [32, 2, 64, 4096], P('date', None, None, 'rng')
Inputs may be any that keep to these rules, and one draw needn't show every extreme that they name: along_track_line_groups[d, g] is strictly increasing: the ingested rows that give the 64 window rows of date d in range segment g. `sweep_identifier`: burst never falls along the rows; each burst holds between 16 and 48 rows.
All inputs are finite; a program needn't handle non-finite values.
Results may differ from a plain program's by a relative error of at most 0.0003.
Values may be sent and summed in bfloat16 or wider, within the bound.
No kernel may reach another device: no remote copies, remote signals or barrier semaphores. Data moves between devices by JAX's collectives and lax.ppermute only.
A program may use at most 128 MiB of HBM per device.

v0:
```python
import jax
import jax.numpy as jnp
from jax import lax
from jax.sharding import PartitionSpec as P

BOX_AZ = 7
BOX_RG = 28
HIGH = lax.Precision.HIGHEST
EPSILON = 1e-06


def from_root(shard, axis, root):
    mine = lax.axis_index(axis) == root
    return lax.psum(jnp.where(mine, shard, jnp.zeros_like(shard)), axis)


def extended(shard, sides, width):
    for axis, dim in sides:
        devices, length = (lax.axis_size(axis), shard.shape[dim])
        up = [(i, (i + 1) % devices) for i in range(devices - 1)]
        down = [(j, i) for i, j in up]
        last = lax.slice_in_dim(shard, length - width, length, axis=dim)
        first = lax.slice_in_dim(shard, 0, width, axis=dim)
        before = lax.ppermute(last, axis, up)
        after = lax.ppermute(first, axis, down)
        shard = jnp.concatenate([before, shard, after], axis=dim)
    return shard


def pick_rows(one_frame, row_index):
    return jnp.take(one_frame, row_index, axis=1)


def features(moving_averaged):
    denominator = jnp.sqrt(moving_averaged[0] * moving_averaged[1]) + EPSILON
    return jnp.stack(
        [
            moving_averaged[2] / denominator,
            moving_averaged[3] / denominator,
            moving_averaged[4] / denominator,
            jnp.log(moving_averaged[1] + EPSILON) - jnp.log(moving_averaged[0] + EPSILON),
            jnp.log(moving_averaged[0] / (BOX_AZ * BOX_RG) + EPSILON),
        ]
    )


def range_band(padded_cols, result_across_lines):
    source_col = lax.broadcasted_iota(jnp.int32, (padded_cols, result_across_lines), 0)
    target_col = lax.broadcasted_iota(jnp.int32, (padded_cols, result_across_lines), 1)
    line_displacement = source_col - target_col
    return ((line_displacement >= 0) & (line_displacement < BOX_RG)).astype(jnp.float32)


def along_track_line_blocks(slant_averaged, sweep_identifier):
    along_track_lines_number = sweep_identifier.shape[0]
    block_line_number = min(128, along_track_lines_number)
    midway_line_number = (BOX_AZ - 1) // 2
    bordered_patch = jnp.pad(
        slant_averaged, ((0, 0), (0, 0), (midway_line_number, midway_line_number), (0, 0))
    )
    sweep_border_fill = jnp.pad(
        sweep_identifier, (midway_line_number, midway_line_number), constant_values=-1
    )
    patch_line_extent = block_line_number + 2 * midway_line_number
    target_row = lax.broadcasted_iota(jnp.int32, (block_line_number, patch_line_extent), 0)
    source_row = lax.broadcasted_iota(jnp.int32, (block_line_number, patch_line_extent), 1)
    near_rows = jnp.abs(source_row - midway_line_number - target_row) <= midway_line_number
    band_rows = (near_rows & (sweep_identifier[:, None] == sweep_border_fill[None, :])).astype(
        jnp.float32
    )
    results = jnp.einsum("pq,knqb->knpb", band_rows, bordered_patch, precision=HIGH)
    return results


def moving_average_planes(bordered_patch, sweep_identifier, result_across_lines):
    as_float = bordered_patch.astype(jnp.float32)
    ref_re = as_float[0, 0]
    ref_im = as_float[0, 1]
    sec_re = as_float[1:, 0]
    sec_im = as_float[1:, 1]
    pow_ref = jnp.broadcast_to(ref_re * ref_re + ref_im * ref_im, sec_re.shape)
    pow_sec = sec_re * sec_re + sec_im * sec_im
    cross_re = ref_re * sec_re + ref_im * sec_im
    cross_im = ref_im * sec_re - ref_re * sec_im
    layered_planes = jnp.stack([pow_ref, pow_sec, cross_re, cross_im, jnp.sqrt(pow_ref * pow_sec)])
    slant_averaged = jnp.einsum(
        "knpa,ab->knpb",
        layered_planes,
        range_band(bordered_patch.shape[3], result_across_lines),
        precision=HIGH,
    )
    moving_averaged = along_track_line_blocks(slant_averaged, sweep_identifier)
    return features(moving_averaged)


def conv_taps(field, weights, biases):
    along_track_lines_number = field.shape[2]
    across_track_number = field.shape[3] - 2
    bordered_patch = jnp.pad(field, ((0, 0), (0, 0), (1, 1), (0, 0)))
    cumulative_tally = (
        jnp.zeros(
            (weights.shape[0], field.shape[1], along_track_lines_number, across_track_number),
            jnp.float32,
        )
        + biases[:, None, None, None]
    )
    for tap_a in range(3):
        for tap_b in range(3):
            cumulative_tally = cumulative_tally + jnp.einsum(
                "oi,inpw->onpw",
                weights[:, :, tap_a, tap_b],
                bordered_patch[
                    :,
                    :,
                    tap_a : tap_a + along_track_lines_number,
                    tap_b : tap_b + across_track_number,
                ],
                precision=HIGH,
            )
    return cumulative_tally


def local(
    slave_complex_pixels,
    along_track_line_groups,
    master_epoch_position,
    sweep_identifier,
    initial_filter_kernel,
    initial_filter_shift,
    latter_filter_kernel,
    latter_filter_shift,
):
    date_count = lax.axis_size("date")
    date_index = lax.axis_index("date")
    per_dev = slave_complex_pixels.shape[0] // date_count
    across_track_number = slave_complex_pixels.shape[3]
    chosen = master_epoch_position[0]
    my_lists = along_track_line_groups[:, 0, :]
    lists_here = lax.dynamic_slice_in_dim(my_lists, date_index * per_dev, per_dev, 0)
    arrived = lax.all_to_all(slave_complex_pixels, "date", split_axis=0, concat_axis=2, tiled=True)
    secondary = jax.vmap(pick_rows)(arrived, lists_here)
    local_ref = lax.dynamic_index_in_dim(secondary, chosen % per_dev, 0, keepdims=False)
    ref_frame = from_root(local_ref, "date", chosen // per_dev)
    stacked = jnp.concatenate([ref_frame[None], secondary], 0)
    bordered_patch = extended(stacked, (("rng", 3),), BOX_RG // 2)
    descriptor_lattice = moving_average_planes(
        bordered_patch, sweep_identifier, across_track_number
    )
    descriptor_lattice = extended(descriptor_lattice, (("rng", 3),), 1)
    hidden = jax.nn.relu(conv_taps(descriptor_lattice, initial_filter_kernel, initial_filter_shift))
    hidden = extended(hidden, (("rng", 3),), 1)
    burn_logits = conv_taps(hidden, latter_filter_kernel, latter_filter_shift)
    return jnp.moveaxis(burn_logits, 0, 1)


def solution(mesh):
    placed = (P(None, None, "date", "rng"), P(None, "rng", None), P(), P(), P(), P(), P(), P())
    return jax.shard_map(
        local, mesh=mesh, in_specs=placed, out_specs=P("date", None, None, "rng"), check_vma=False
    )
```

profile of v0, /device:TPU:128, one launch (start us, length us, event | category | flops | bytes accessed | tf_op | source)
XLA Modules:
  0.0 294.7 jit_solution(7778671245150096637)
XLA Ops:
  6.5 7.2 %all-to-all-start = ((bf16[32,2,8,256]{3,2,1,0:T(8,128)(2,1)}), bf16[32,2,8,256]{3,2,1,0:T(8,128)(2,1)S(1)}, u32[]{:S(2)}, u32[]{:S(2)}) async-start(bf16[32,2,8,256]{3,2,1,0:T(8,128)(2,1)} %param.8), calls=%async_computation | async-start | bytes 524288 | tf_op jit(solution)/shard_map/all_to_all | solution.py:140
  13.7 0.0 all-reduce.6.cloned.1.call-start
  14.5 0.1 reshape.128
  14.6 0.9 fusion.117
  15.5 7.4 %all-to-all-done = bf16[32,2,8,256]{3,2,1,0:T(8,128)(2,1)S(1)} async-done(((bf16[32,2,8,256]{3,2,1,0:T(8,128)(2,1)}), bf16[32,2,8,256]{3,2,1,0:T(8,128)(2,1)S(1)}, u32[]{:S(2)}, u32[]{:S(2)}) %all-to-all-start) | async-done | bytes 262176 | tf_op jit(solution)/shard_map/all_to_all | solution.py:140
  22.9 0.3 copy.74
  23.2 1.0 gather_fusion
  24.2 0.1 broadcast_select_fusion
  24.3 0.6 select_bitcast_fusion
  25.0 0.0 all-reduce.6.cloned.1.call-update
  25.0 0.1 fusion.120
  25.1 131.5 %all-reduce.6.cloned.1.call-done = bf16[1,2,64,256]{3,2,0,1:T(8,128)(2,1)} async-done(((bf16[1,2,64,256]{3,2,0,1:T(8,128)(2,1)}), bf16[1,2,64,256]{3,2,0,1:T(8,128)(2,1)}) %all-reduce.6.cloned.1.call-update) | async-done | bytes 65552 | tf_op jit(solution)/shard_map/psum | solution.py:14
  156.6 0.9 fusion.77
  157.4 3.4 %collective-permute-start = (bf16[3,2,64,14]{3,2,0,1:T(8,128)(2,1)S(1)}, bf16[3,2,64,14]{3,2,0,1:T(8,128)(2,1)S(1)}, u32[]{:S(2)}, u32[]{:S(2)}) collective-permute-start(bf16[3,2,64,14]{3,2,0,1:T(8,128)(2,1)S(1)} %get-tuple-element.23), channel_id=1, source_target_pairs={{0,1},{1,2},{2,3},{3,4},{4,5},{5,6},{6,7},{7,8},{8,9},{9,10},{10,1... | collective-permute-start | bytes 32264 | tf_op jit(solution)/shard_map/ppermute | solution.py:24
  160.8 4.6 %collective-permute-start.1 = (bf16[3,2,64,14]{3,2,0,1:T(8,128)(2,1)S(1)}, bf16[3,2,64,14]{3,2,0,1:T(8,128)(2,1)S(1)}, u32[]{:S(2)}, u32[]{:S(2)}) collective-permute-start(bf16[3,2,64,14]{3,2,0,1:T(8,128)(2,1)S(1)} %get-tuple-element.24), channel_id=1, source_target_pairs={{1,0},{2,1},{3,2},{4,3},{5,4},{6,5},{7,6},{8,7},{9,8},{10,9},{11,1... | collective-permute-start | bytes 32264 | tf_op jit(solution)/shard_map/ppermute | solution.py:25
  165.4 0.7 pad.17
  166.1 1.4 collective-permute-done.1
  167.6 0.9 multiply_add_fusion
  168.5 0.1 fusion.71
  168.7 0.1 sqrt_dynamic-update-slice_fusion
  168.8 0.7 fusion.60
  169.6 0.6 convolution_bitcast_fusion
  170.1 0.1 fusion.76
  170.2 0.1 fusion.75
  170.3 0.1 fusion.74
  170.4 0.2 fusion.116
  170.6 3.2 %collective-permute-start.2 = (f32[5,2,64,1]{3,2,1,0:T(8,128)S(1)}, f32[5,2,64,1]{3,2,1,0:T(8,128)S(1)}, u32[]{:S(2)}, u32[]{:S(2)}) collective-permute-start(f32[5,2,64,1]{3,2,1,0:T(8,128)S(1)} %get-tuple-element.21), channel_id=1, source_target_pairs={{0,1},{1,2},{2,3},{3,4},{4,5},{5,6},{6,7},{7,8},{8,9},{9,10},{10,1... | collective-permute-start | bytes 7688 | tf_op jit(solution)/shard_map/ppermute | solution.py:24
  173.8 5.3 %collective-permute-start.3 = (f32[5,2,64,1]{3,2,1,0:T(8,128)S(1)}, f32[5,2,64,1]{3,2,1,0:T(8,128)S(1)}, u32[]{:S(2)}, u32[]{:S(2)}) collective-permute-start(f32[5,2,64,1]{3,2,1,0:T(8,128)S(1)} %get-tuple-element.22), channel_id=1, source_target_pairs={{1,0},{2,1},{3,2},{4,3},{5,4},{6,5},{7,6},{8,7},{9,8},{10,9},{11,1... | collective-permute-start | bytes 7688 | tf_op jit(solution)/shard_map/ppermute | solution.py:25
  179.1 3.6 %fusion.45 = f32[2,64,256,32]{2,3,1,0:T(8,128)S(1)} fusion(f32[5,2,64,256]{3,2,1,0:T(8,128)S(1)} %log_dynamic-update-slice_fusion, f32[32,5,1,1]{0,3,2,1:T(1,128)S(1)} %get-tuple-element.28), kind=kOutput, calls=%fused_computation.48 | convolution fusion | flops 62914560 | bytes 4850304 | tf_op jit(solution)/shard_map/oi,inpw->onpw/dot_general | solution.py:109
  182.7 2.1 collective-permute-done.2
  184.8 3.9 %collective-permute-done.3 = f32[5,2,64,1]{3,2,1,0:T(8,128)S(1)} collective-permute-done((f32[5,2,64,1]{3,2,1,0:T(8,128)S(1)}, f32[5,2,64,1]{3,2,1,0:T(8,128)S(1)}, u32[]{:S(2)}, u32[]{:S(2)}) %collective-permute-start.3) | collective-permute-done | bytes 2592 | tf_op jit(solution)/shard_map/ppermute | solution.py:25
  188.7 0.5 select_maximum_fusion.2
  189.2 0.8 fusion.115
  190.0 3.6 %fusion.53 = f32[2,64,256,32]{2,3,1,0:T(8,128)S(1)} fusion(f32[5,2,64,256]{3,2,1,0:T(8,128)S(1)} %get-tuple-element.13, f32[32,5,1,1]{0,3,2,1:T(1,128)S(1)} %get-tuple-element.32), kind=kOutput, calls=%fused_computation.56 | convolution fusion | flops 62914560 | bytes 4850304 | tf_op jit(solution)/shard_map/oi,inpw->onpw/dot_general | solution.py:109
  193.5 3.6 %fusion.40 = f32[2,64,256,32]{2,3,1,0:T(8,128)S(1)} fusion(f32[5,2,64,256]{3,2,1,0:T(8,128)S(1)} %get-tuple-element.14, f32[32,5,1,1]{0,3,2,1:T(1,128)S(1)} %get-tuple-element.26), kind=kOutput, calls=%fused_computation.43 | convolution fusion | flops 62914560 | bytes 4850304 | tf_op jit(solution)/shard_map/oi,inpw->onpw/dot_general | solution.py:109
  197.1 5.3 %fusion.42 = f32[2,64,256,32]{2,3,1,0:T(8,128)} fusion(f32[5,2,64,256]{3,2,1,0:T(8,128)S(1)} %get-tuple-element.15, f32[32,5,1,1]{0,3,2,1:T(1,128)S(1)} %get-tuple-element.27), kind=kOutput, calls=%fused_computation.45 | convolution fusion | flops 62914560 | bytes 4850304 | tf_op jit(solution)/shard_map/oi,inpw->onpw/dot_general | solution.py:109
  202.4 5.0 %fusion.49 = f32[2,64,256,32]{2,3,1,0:T(8,128)} fusion(f32[5,2,64,256]{3,2,1,0:T(8,128)S(1)} %get-tuple-element.16, f32[32,5,1,1]{0,3,2,1:T(1,128)S(1)} %get-tuple-element.30), kind=kOutput, calls=%fused_computation.52 | convolution fusion | flops 62914560 | bytes 4850304 | tf_op jit(solution)/shard_map/oi,inpw->onpw/dot_general | solution.py:109
  207.5 5.1 %fusion.51 = f32[2,64,256,32]{2,3,1,0:T(8,128)} fusion(f32[5,2,64,256]{3,2,1,0:T(8,128)S(1)} %get-tuple-element.17, f32[32,5,1,1]{0,3,2,1:T(1,128)S(1)} %get-tuple-element.31), kind=kOutput, calls=%fused_computation.54 | convolution fusion | flops 62914560 | bytes 4850304 | tf_op jit(solution)/shard_map/oi,inpw->onpw/dot_general | solution.py:109
  212.5 5.0 %fusion.38 = f32[2,64,256,32]{2,3,1,0:T(8,128)} fusion(f32[5,2,64,256]{3,2,1,0:T(8,128)S(1)} %get-tuple-element.18, f32[32,5,1,1]{0,3,2,1:T(1,128)S(1)} %get-tuple-element.33), kind=kOutput, calls=%fused_computation.41 | convolution fusion | flops 62914560 | bytes 4850304 | tf_op jit(solution)/shard_map/oi,inpw->onpw/dot_general | solution.py:109
  217.6 0.5 pad_maximum_fusion.14
  218.1 5.0 %fusion.47 = f32[2,64,256,32]{2,3,1,0:T(8,128)} fusion(f32[5,2,64,256]{3,2,1,0:T(8,128)S(1)} %get-tuple-element.20, f32[32,5,1,1]{0,3,2,1:T(1,128)S(1)} %get-tuple-element.29), kind=kOutput, calls=%fused_computation.50 | convolution fusion | flops 62914560 | bytes 4850304 | tf_op jit(solution)/shard_map/oi,inpw->onpw/dot_general | solution.py:109
  223.1 10.2 %maximum_bitcast_fusion = f32[32,2,64,256]{3,0,2,1:T(8,128)S(1)} fusion(f32[2,64,256,32]{2,3,1,0:T(8,128)} %fusion.38, f32[2,64,256,32]{2,3,1,0:T(8,128)S(1)} %fusion.40, f32[2,64,256,32]{2,3,1,0:T(8,128)} %fusion.42, f32[2,64,256,32]{2,3,1,0:T(8,128)S(1)} %fusion.45, f32[2,64,256,32]{2,3,1,0:T(8,128)} %fusion.47, f32[2,64,256,32]{2,3,1,0:T(8,128)} %fusion.49, ...), kind=kOutput, calls=%fused_computation.24 | convolution fusion | flops 73400320 | bytes 38404864 | tf_op jit(solution)/shard_map/oi,inpw->onpw/dot_general | solution.py:109
  233.3 0.0 copy-start.6
  233.3 3.2 %fusion.114 = (f32[32,2,64,1]{3,0,2,1:T(8,128)}, f32[32,2,64,1]{3,0,2,1:T(8,128)}) fusion(f32[32,2,64,256]{3,0,2,1:T(8,128)S(1)} %maximum_bitcast_fusion), kind=kLoop, calls=%fused_computation.148 | loop fusion | bytes 65536 | tf_op jit(solution)/shard_map/slice | solution.py:22
  236.5 0.1 copy-done.2
  236.6 2.8 copy.95
  239.4 2.3 collective-permute-start.4
  241.7 4.5 %fusion.102 = f32[2,64,256,2]{2,3,1,0:T(2,128)S(1)} fusion(f32[32,2,64,256]{3,0,2,1:T(8,128)} %copy-done.2, f32[2,32,3,3]{1,0,3,2:T(2,128)S(1)} %copy-done.6), kind=kOutput, calls=%fused_computation.134 | convolution fusion | flops 25165824 | bytes 4457472 | tf_op jit(solution)/shard_map/oi,inpw->onpw/dot_general | solution.py:109
  246.2 1.1 copy.96
  247.3 6.0 %collective-permute-start.5 = (f32[32,2,64,1]{2,0,3,1:T(8,128)S(1)}, f32[32,2,64,1]{2,0,3,1:T(8,128)S(1)}, u32[]{:S(2)}, u32[]{:S(2)}) collective-permute-start(f32[32,2,64,1]{2,0,3,1:T(8,128)S(1)} %copy.96), channel_id=1, source_target_pairs={{1,0},{2,1},{3,2},{4,3},{5,4},{6,5},{7,6},{8,7},{9,8},{10,9},{11,1... | collective-permute-start | bytes 49160 | tf_op jit(solution)/shard_map/ppermute | solution.py:25
  253.4 1.9 copy.97
  255.2 4.9 %fusion.9 = f32[2,64,256,2]{2,3,1,0:T(2,128)S(1)} fusion(f32[32,2,64,256]{3,0,2,1:T(8,128)} %copy-done.2, f32[32,2,64,1]{3,0,2,1:T(8,128)S(1)} %copy.97, f32[2,32,3,3]{1,0,3,2:T(2,128)S(1)} %copy-done.6), kind=kOutput, calls=%fused_computation.16 | convolution fusion | flops 26214400 | bytes 6554624 | tf_op jit(solution)/shard_map/oi,inpw->onpw/dot_general | solution.py:109
  260.1 2.9 copy.98
  263.1 5.0 %select_maximum_fusion = f32[32,2,66,258]{3,0,2,1:T(8,128)S(1)} fusion(f32[32,2,64,1]{3,0,2,1:T(8,128)} %copy.98, f32[32,2,64,256]{3,0,2,1:T(8,128)} %copy-done.2, f32[32,2,64,1]{3,0,2,1:T(8,128)S(1)} %copy.97), kind=kLoop, calls=%fused_computation.3 | loop fusion | flops 8718336 | bytes 8586240 | tf_op jit(solution)/shard_map/concatenate | solution.py:26
  268.0 2.6 fusion.3
  270.7 2.3 fusion.5
  273.0 2.6 fusion.11
  275.6 0.0 copy-start.8
  275.6 2.6 fusion.13
  278.3 2.9 fusion.1
  281.2 0.0 copy-start.1
  281.2 2.4 fusion.34
  283.6 3.3 %fusion.27 = f32[2,2,64,256]{3,1,2,0:T(2,128)S(1)} fusion(f32[2,64,256,2]{2,3,1,0:T(2,128)S(1)} %fusion.1, f32[2,64,256,2]{2,3,1,0:T(2,128)S(1)} %fusion.3, f32[2,64,256,2]{2,3,1,0:T(2,128)S(1)} %fusion.5, f32[2,64,256,2]{2,3,1,0:T(2,128)S(1)} %fusion.34, f32[32,2,64,1]{3,0,2,1:T(8,128)S(1)} %copy-done.4, f32[32,2,64,256]{3,0,2,1:T(8,128)S(1)} %copy-done.3, ...), kind=kOutput, calls=%fused_computation.34 | convolution fusion | flops 26476544 | bytes 7603200 | tf_op jit(solution)/shard_map/oi,inpw->onpw/dot_general | solution.py:109
  286.9 0.7 copy.101
  (30 shorter events, 0.3 us)
Async XLA Ops:
  6.5 7.2 %copy-start = (s32[32,1,64]{2,1,0:T(1,128)S(1)}, s32[32,1,64]{2,1,0:T(1,128)}, u32[]{:S(2)}) copy-start(s32[32,1,64]{2,1,0:T(1,128)} %param.9) | copy-start | bytes 24580
  6.5 163.0 %copy-start.9 = (s32[64]{0:T(128)S(1)}, s32[64]{0:T(128)}, u32[]{:S(2)}) copy-start(s32[64]{0:T(128)} %param.11) | copy-start | bytes 772
  6.5 16.3 %all-to-all-start = ((bf16[32,2,8,256]{3,2,1,0:T(8,128)(2,1)}), bf16[32,2,8,256]{3,2,1,0:T(8,128)(2,1)S(1)}, u32[]{:S(2)}, u32[]{:S(2)}) async-start(bf16[32,2,8,256]{3,2,1,0:T(8,128)(2,1)} %param.8), calls=%async_computation | async-start | bytes 524288 | tf_op jit(solution)/shard_map/all_to_all | solution.py:140
  13.7 142.8 %all-reduce.6.cloned.1.call-start = ((), (), s32[]{:S(2)}) async-start(), calls=%async_computation.1 | async-start | bytes 131072 | tf_op jit(solution)/shard_map/psum | solution.py:14
  157.4 8.7 %collective-permute-start = (bf16[3,2,64,14]{3,2,0,1:T(8,128)(2,1)S(1)}, bf16[3,2,64,14]{3,2,0,1:T(8,128)(2,1)S(1)}, u32[]{:S(2)}, u32[]{:S(2)}) collective-permute-start(bf16[3,2,64,14]{3,2,0,1:T(8,128)(2,1)S(1)} %get-tuple-element.23), channel_id=1, source_target_pairs={{0,1},{1,2},{2,3},{3,4},{4,5},{5,6},{6,7},{7,8},{8,9},{9,10},{10,1... | collective-permute-start | bytes 32264 | tf_op jit(solution)/shard_map/ppermute | solution.py:24
  160.8 6.8 %collective-permute-start.1 = (bf16[3,2,64,14]{3,2,0,1:T(8,128)(2,1)S(1)}, bf16[3,2,64,14]{3,2,0,1:T(8,128)(2,1)S(1)}, u32[]{:S(2)}, u32[]{:S(2)}) collective-permute-start(bf16[3,2,64,14]{3,2,0,1:T(8,128)(2,1)S(1)} %get-tuple-element.24), channel_id=1, source_target_pairs={{1,0},{2,1},{3,2},{4,3},{5,4},{6,5},{7,6},{8,7},{9,8},{10,9},{11,1... | collective-permute-start | bytes 32264 | tf_op jit(solution)/shard_map/ppermute | solution.py:25
  170.6 14.2 %collective-permute-start.2 = (f32[5,2,64,1]{3,2,1,0:T(8,128)S(1)}, f32[5,2,64,1]{3,2,1,0:T(8,128)S(1)}, u32[]{:S(2)}, u32[]{:S(2)}) collective-permute-start(f32[5,2,64,1]{3,2,1,0:T(8,128)S(1)} %get-tuple-element.21), channel_id=1, source_target_pairs={{0,1},{1,2},{2,3},{3,4},{4,5},{5,6},{6,7},{7,8},{8,9},{9,10},{10,1... | collective-permute-start | bytes 7688 | tf_op jit(solution)/shard_map/ppermute | solution.py:24
  173.8 14.9 %collective-permute-start.3 = (f32[5,2,64,1]{3,2,1,0:T(8,128)S(1)}, f32[5,2,64,1]{3,2,1,0:T(8,128)S(1)}, u32[]{:S(2)}, u32[]{:S(2)}) collective-permute-start(f32[5,2,64,1]{3,2,1,0:T(8,128)S(1)} %get-tuple-element.22), channel_id=1, source_target_pairs={{1,0},{2,1},{3,2},{4,3},{5,4},{6,5},{7,6},{8,7},{9,8},{10,9},{11,1... | collective-permute-start | bytes 7688 | tf_op jit(solution)/shard_map/ppermute | solution.py:25
  217.6 5.5 %copy-start.7 = (f32[32]{0:T(128)S(1)}, f32[32]{0:T(128)}, u32[]{:S(2)}) copy-start(f32[32]{0:T(128)} %param.13) | copy-start | bytes 388
  233.3 3.3 %copy-start.2 = (f32[32,2,64,256]{3,0,2,1:T(8,128)}, f32[32,2,64,256]{3,0,2,1:T(8,128)S(1)}, u32[]{:S(2)}) copy-start(f32[32,2,64,256]{3,0,2,1:T(8,128)S(1)} %maximum_bitcast_fusion) | copy-start | bytes 12582916
  233.3 8.4 %copy-start.6 = (f32[2,32,3,3]{1,0,3,2:T(2,128)S(1)}, f32[2,32,3,3]{1,0,3,2:T(2,128)}, u32[]{:S(2)}) copy-start(f32[2,32,3,3]{1,0,3,2:T(2,128)} %param.14) | copy-start | bytes 6916
  236.6 9.6 %copy-start.5 = (f32[32,2,64,1]{3,0,2,1:T(8,128)S(1)}, f32[32,2,64,1]{3,0,2,1:T(8,128)}, u32[]{:S(2)}) copy-start(f32[32,2,64,1]{3,0,2,1:T(8,128)} %get-tuple-element.12) | copy-start | bytes 49156
  239.4 14.0 %collective-permute-start.4 = (f32[32,2,64,1]{2,0,3,1:T(8,128)S(1)}, f32[32,2,64,1]{2,0,3,1:T(8,128)S(1)}, u32[]{:S(2)}, u32[]{:S(2)}) collective-permute-start(f32[32,2,64,1]{2,0,3,1:T(8,128)S(1)} %copy.95), channel_id=1, source_target_pairs={{0,1},{1,2},{2,3},{3,4},{4,5},{5,6},{6,7},{7,8},{8,9},{9,10},{10,1... | collective-permute-start | bytes 49160 | tf_op jit(solution)/shard_map/ppermute | solution.py:24
  247.3 12.8 %collective-permute-start.5 = (f32[32,2,64,1]{2,0,3,1:T(8,128)S(1)}, f32[32,2,64,1]{2,0,3,1:T(8,128)S(1)}, u32[]{:S(2)}, u32[]{:S(2)}) collective-permute-start(f32[32,2,64,1]{2,0,3,1:T(8,128)S(1)} %copy.96), channel_id=1, source_target_pairs={{1,0},{2,1},{3,2},{4,3},{5,4},{6,5},{7,6},{8,7},{9,8},{10,9},{11,1... | collective-permute-start | bytes 49160 | tf_op jit(solution)/shard_map/ppermute | solution.py:25
  275.6 5.5 %copy-start.8 = (f32[2]{0:T(128)S(1)}, f32[2]{0:T(128)}, u32[]{:S(2)}) copy-start(f32[2]{0:T(128)} %param.15) | copy-start | bytes 28
  278.3 5.3 %copy-start.3 = (f32[32,2,64,256]{3,0,2,1:T(8,128)S(1)}, f32[32,2,64,256]{3,0,2,1:T(8,128)}, u32[]{:S(2)}) copy-start(f32[32,2,64,256]{3,0,2,1:T(8,128)} %copy-done.2) | copy-start | bytes 12582916
  278.3 5.3 %copy-start.4 = (f32[32,2,64,1]{3,0,2,1:T(8,128)S(1)}, f32[32,2,64,1]{3,0,2,1:T(8,128)}, u32[]{:S(2)}) copy-start(f32[32,2,64,1]{3,0,2,1:T(8,128)} %copy.98) | copy-start | bytes 49156
  281.2 6.5 %copy-start.1 = (s32[32,1,64]{2,1,0:T(1,128)S(1)}, s32[32,1,64]{2,1,0:T(1,128)}, u32[]{:S(2)}) copy-start(s32[32,1,64]{2,1,0:T(1,128)} %param.9) | copy-start | bytes 24580
Sparse Core Ops, SparseCore 0:
  25.1 131.4 all-reduce.5
where the time goes:
time: 299 us; the launch traced here: 295 us
  waiting for transfers between devices  146 us (49%)
  matrix products  75.8 us (25%)
  starting transfers between devices  32 us (11%)
  local copies, waits for them, and re-layouts  16.7 us (6%)
  between operations  14.8 us (5%)
  other arithmetic  9.08 us (3%)
    psum x1, waiting for transfers between devices, from_root(): return lax.psum(jnp.where(mine, shard, jnp.zeros_like(shard)), axis)  131 us
    dot_general x18, matrix products, conv_taps(): jnp.einsum('oi,inpw->onpw', weights[:, :, tap_a, tap_b], bordered_patch[:...  74.5 us
    ppermute x3, starting transfers between devices, extended(): after = lax.ppermute(first, axis, down)  15.9 us
    ppermute x3, starting transfers between devices, extended(): before = lax.ppermute(last, axis, up)  8.91 us
    all_to_all x1, waiting for transfers between devices, local(): lax.all_to_all(slave_complex_pixels, 'date', split_axis=0, concat_axis=2,...  7.41 us
    all_to_all x1, starting transfers between devices, local(): lax.all_to_all(slave_complex_pixels, 'date', split_axis=0, concat_axis=2,...  7.17 us
    slice x3, local copies, waits for them, and re-layouts, extended(): last = lax.slice_in_dim(shard, length - width, length, axis=dim)  6.1 us
  transfers between devices with their start and end apart: 8, of which 5 were waited for; matrix products, arithmetic and copies ran while one was open for 6% of the time, Pallas kernels for 0%

commit v1 on v0

--- a/solution.py
+++ b/solution.py
@@ -9,9 +9,15 @@
 EPSILON = 1e-06
 
 
+def gather_and_add(shard, axis):
+    pieces = lax.all_gather(shard, axis, axis=0, tiled=False)
+    result = pieces.sum(axis=0)
+    return result
+
+
 def from_root(shard, axis, root):
     mine = lax.axis_index(axis) == root
-    return lax.psum(jnp.where(mine, shard, jnp.zeros_like(shard)), axis)
+    return gather_and_add(jnp.where(mine, shard, jnp.zeros_like(shard)), axis)
 
 
 def extended(shard, sides, width):

time: 299 us -> 218 us (0.73)
  waiting for transfers between devices: 146 us -> 66.5 us
    psum x1 -> x0, waiting for transfers between devices: 131 us -> none  [from_root(): return lax.psum(jnp.where(mine, shard, jnp.zeros_like(shard)), axis)]
    all_gather x0 -> x1, waiting for transfers between devices: none -> 46.4 us  [gather_and_add(): pieces = lax.all_gather(shard, axis, axis=0, tiled=False)]
    ppermute x3, waiting for transfers between devices: 2.13 us -> 5.61 us  [extended(): before = lax.ppermute(last, axis, up)]
  transfers between devices with their start and end apart: 8 -> 8, of which waited for: 5 -> 6; matrix products, arithmetic and copies ran while one was open for 6% -> 8% of each run, Pallas kernels for 0% -> 0%
where the time goes in v1:
time: 218 us; the launch traced here: 214 us
  matrix products  75.8 us (35%)
  waiting for transfers between devices  66.5 us (31%)
  starting transfers between devices  31.6 us (14%)
  local copies, waits for them, and re-layouts  16.1 us (7%)
  between operations  14.8 us (7%)
  other arithmetic  8.89 us (4%)
    dot_general x18, matrix products, conv_taps(): jnp.einsum('oi,inpw->onpw', weights[:, :, tap_a, tap_b], bordered_patch[:...  74.5 us
    all_gather x1, waiting for transfers between devices, gather_and_add(): pieces = lax.all_gather(shard, axis, axis=0, tiled=False)  46.4 us
    ppermute x3, starting transfers between devices, extended(): after = lax.ppermute(first, axis, down)  17.3 us
    all_to_all x1, waiting for transfers between devices, local(): lax.all_to_all(slave_complex_pixels, 'date', split_axis=0, concat_axis=2,...  8.3 us
    all_to_all x1, starting transfers between devices, local(): lax.all_to_all(slave_complex_pixels, 'date', split_axis=0, concat_axis=2,...  7.17 us
    ppermute x3, starting transfers between devices, extended(): before = lax.ppermute(last, axis, up)  7.16 us
    ppermute x3, waiting for transfers between devices, extended(): after = lax.ppermute(first, axis, down)  6.13 us
    slice x3, local copies, waits for them, and re-layouts, extended(): last = lax.slice_in_dim(shard, length - width, length, axis=dim)  6.1 us
  transfers between devices with their start and end apart: 8, of which 6 were waited for; matrix products, arithmetic and copies ran while one was open for 8% of the time, Pallas kernels for 0%

profile of v1, /device:TPU:128, one launch (start us, length us, event | category | flops | bytes accessed | tf_op | source)
XLA Modules:
  0.0 213.6 jit_solution(9792612346393666871)
XLA Ops:
  6.5 7.2 %all-to-all-start = ((bf16[32,2,8,256]{3,2,1,0:T(8,128)(2,1)}), bf16[32,2,8,256]{3,2,1,0:T(8,128)(2,1)S(1)}, u32[]{:S(2)}, u32[]{:S(2)}) async-start(bf16[32,2,8,256]{3,2,1,0:T(8,128)(2,1)} %param.8), calls=%async_computation | async-start | bytes 524288 | tf_op jit(solution)/shard_map/all_to_all | solution.py:146
  13.7 0.0 all-gather.2.cloned.1.call-start
  14.5 0.1 reshape.124
  14.6 8.3 %all-to-all-done = bf16[32,2,8,256]{3,2,1,0:T(8,128)(2,1)S(1)} async-done(((bf16[32,2,8,256]{3,2,1,0:T(8,128)(2,1)}), bf16[32,2,8,256]{3,2,1,0:T(8,128)(2,1)S(1)}, u32[]{:S(2)}, u32[]{:S(2)}) %all-to-all-start) | async-done | bytes 262176 | tf_op jit(solution)/shard_map/all_to_all | solution.py:146
  22.9 0.3 copy.74
  23.2 1.0 gather_fusion
  24.2 0.1 broadcast_select_fusion
  24.3 0.6 select_bitcast_fusion
  25.0 0.0 all-gather.2.cloned.1.call-update
  25.0 0.9 fusion.117
  25.9 0.1 fusion.120
  26.0 46.4 %all-gather.2.cloned.1.call-done = bf16[16,2,64,256]{3,2,0,1:T(8,128)(2,1)} async-done(((bf16[1,2,64,256]{3,2,0,1:T(8,128)(2,1)}), bf16[16,2,64,256]{3,2,0,1:T(8,128)(2,1)}) %all-gather.2.cloned.1.call-update) | async-done | bytes 1048592 | tf_op jit(solution)/shard_map/all_gather | solution.py:13
  72.4 1.4 reduce_sum.12
  73.7 0.1 fusion.77
  73.8 2.5 %collective-permute-start = (bf16[3,2,64,14]{3,2,0,1:T(8,128)(2,1)S(1)}, bf16[3,2,64,14]{3,2,0,1:T(8,128)(2,1)S(1)}, u32[]{:S(2)}, u32[]{:S(2)}) collective-permute-start(bf16[3,2,64,14]{3,2,0,1:T(8,128)(2,1)S(1)} %get-tuple-element.23), channel_id=1, source_target_pairs={{0,1},{1,2},{2,3},{3,4},{4,5},{5,6},{6,7},{7,8},{8,9},{9,10},{10,1... | collective-permute-start | bytes 32264 | tf_op jit(solution)/shard_map/ppermute | solution.py:30
  76.3 5.5 %collective-permute-start.1 = (bf16[3,2,64,14]{3,2,0,1:T(8,128)(2,1)S(1)}, bf16[3,2,64,14]{3,2,0,1:T(8,128)(2,1)S(1)}, u32[]{:S(2)}, u32[]{:S(2)}) collective-permute-start(bf16[3,2,64,14]{3,2,0,1:T(8,128)(2,1)S(1)} %get-tuple-element.24), channel_id=1, source_target_pairs={{1,0},{2,1},{3,2},{4,3},{5,4},{6,5},{7,6},{8,7},{9,8},{10,9},{11,1... | collective-permute-start | bytes 32264 | tf_op jit(solution)/shard_map/ppermute | solution.py:31
  81.8 0.1 pad.17
  81.9 1.0 collective-permute-done
  82.9 2.0 collective-permute-done.1
  84.9 0.1 multiply_add_fusion
  85.0 0.1 fusion.71
  85.3 0.1 sqrt_dynamic-update-slice_fusion
  85.3 0.7 fusion.60
  86.0 0.6 convolution_bitcast_fusion
  86.6 0.1 fusion.76
  86.7 0.1 fusion.75
  86.8 0.1 fusion.74
  86.9 0.2 fusion.116
  87.1 2.4 %collective-permute-start.2 = (f32[5,2,64,1]{3,2,1,0:T(8,128)S(1)}, f32[5,2,64,1]{3,2,1,0:T(8,128)S(1)}, u32[]{:S(2)}, u32[]{:S(2)}) collective-permute-start(f32[5,2,64,1]{3,2,1,0:T(8,128)S(1)} %get-tuple-element.21), channel_id=1, source_target_pairs={{0,1},{1,2},{2,3},{3,4},{4,5},{5,6},{6,7},{7,8},{8,9},{9,10},{10,1... | collective-permute-start | bytes 7688 | tf_op jit(solution)/shard_map/ppermute | solution.py:30
  89.4 5.8 %collective-permute-start.3 = (f32[5,2,64,1]{3,2,1,0:T(8,128)S(1)}, f32[5,2,64,1]{3,2,1,0:T(8,128)S(1)}, u32[]{:S(2)}, u32[]{:S(2)}) collective-permute-start(f32[5,2,64,1]{3,2,1,0:T(8,128)S(1)} %get-tuple-element.22), channel_id=1, source_target_pairs={{1,0},{2,1},{3,2},{4,3},{5,4},{6,5},{7,6},{8,7},{9,8},{10,9},{11,1... | collective-permute-start | bytes 7688 | tf_op jit(solution)/shard_map/ppermute | solution.py:31
  95.2 3.6 %fusion.45 = f32[2,64,256,32]{2,3,1,0:T(8,128)S(1)} fusion(f32[5,2,64,256]{3,2,1,0:T(8,128)S(1)} %log_dynamic-update-slice_fusion, f32[32,5,1,1]{0,3,2,1:T(1,128)S(1)} %get-tuple-element.28), kind=kOutput, calls=%fused_computation.48 | convolution fusion | flops 62914560 | bytes 4850304 | tf_op jit(solution)/shard_map/oi,inpw->onpw/dot_general | solution.py:115
  98.8 4.6 %collective-permute-done.2 = f32[5,2,64,1]{3,2,1,0:T(8,128)S(1)} collective-permute-done((f32[5,2,64,1]{3,2,1,0:T(8,128)S(1)}, f32[5,2,64,1]{3,2,1,0:T(8,128)S(1)}, u32[]{:S(2)}, u32[]{:S(2)}) %collective-permute-start.2) | collective-permute-done | bytes 2592 | tf_op jit(solution)/shard_map/ppermute | solution.py:30
  103.4 4.1 %collective-permute-done.3 = f32[5,2,64,1]{3,2,1,0:T(8,128)S(1)} collective-permute-done((f32[5,2,64,1]{3,2,1,0:T(8,128)S(1)}, f32[5,2,64,1]{3,2,1,0:T(8,128)S(1)}, u32[]{:S(2)}, u32[]{:S(2)}) %collective-permute-start.3) | collective-permute-done | bytes 2592 | tf_op jit(solution)/shard_map/ppermute | solution.py:31
  107.6 0.5 select_maximum_fusion.2
  108.0 0.8 fusion.115
  108.8 3.6 %fusion.53 = f32[2,64,256,32]{2,3,1,0:T(8,128)S(1)} fusion(f32[5,2,64,256]{3,2,1,0:T(8,128)S(1)} %get-tuple-element.13, f32[32,5,1,1]{0,3,2,1:T(1,128)S(1)} %get-tuple-element.32), kind=kOutput, calls=%fused_computation.56 | convolution fusion | flops 62914560 | bytes 4850304 | tf_op jit(solution)/shard_map/oi,inpw->onpw/dot_general | solution.py:115
  112.4 3.6 %fusion.40 = f32[2,64,256,32]{2,3,1,0:T(8,128)S(1)} fusion(f32[5,2,64,256]{3,2,1,0:T(8,128)S(1)} %get-tuple-element.14, f32[32,5,1,1]{0,3,2,1:T(1,128)S(1)} %get-tuple-element.26), kind=kOutput, calls=%fused_computation.43 | convolution fusion | flops 62914560 | bytes 4850304 | tf_op jit(solution)/shard_map/oi,inpw->onpw/dot_general | solution.py:115
  116.0 5.3 %fusion.42 = f32[2,64,256,32]{2,3,1,0:T(8,128)} fusion(f32[5,2,64,256]{3,2,1,0:T(8,128)S(1)} %get-tuple-element.15, f32[32,5,1,1]{0,3,2,1:T(1,128)S(1)} %get-tuple-element.27), kind=kOutput, calls=%fused_computation.45 | convolution fusion | flops 62914560 | bytes 4850304 | tf_op jit(solution)/shard_map/oi,inpw->onpw/dot_general | solution.py:115
  121.3 5.0 %fusion.49 = f32[2,64,256,32]{2,3,1,0:T(8,128)} fusion(f32[5,2,64,256]{3,2,1,0:T(8,128)S(1)} %get-tuple-element.16, f32[32,5,1,1]{0,3,2,1:T(1,128)S(1)} %get-tuple-element.30), kind=kOutput, calls=%fused_computation.52 | convolution fusion | flops 62914560 | bytes 4850304 | tf_op jit(solution)/shard_map/oi,inpw->onpw/dot_general | solution.py:115
  126.3 5.1 %fusion.51 = f32[2,64,256,32]{2,3,1,0:T(8,128)} fusion(f32[5,2,64,256]{3,2,1,0:T(8,128)S(1)} %get-tuple-element.17, f32[32,5,1,1]{0,3,2,1:T(1,128)S(1)} %get-tuple-element.31), kind=kOutput, calls=%fused_computation.54 | convolution fusion | flops 62914560 | bytes 4850304 | tf_op jit(solution)/shard_map/oi,inpw->onpw/dot_general | solution.py:115
  131.4 5.0 %fusion.38 = f32[2,64,256,32]{2,3,1,0:T(8,128)} fusion(f32[5,2,64,256]{3,2,1,0:T(8,128)S(1)} %get-tuple-element.18, f32[32,5,1,1]{0,3,2,1:T(1,128)S(1)} %get-tuple-element.33), kind=kOutput, calls=%fused_computation.41 | convolution fusion | flops 62914560 | bytes 4850304 | tf_op jit(solution)/shard_map/oi,inpw->onpw/dot_general | solution.py:115
  136.4 0.5 pad_maximum_fusion.14
  136.9 5.0 %fusion.47 = f32[2,64,256,32]{2,3,1,0:T(8,128)} fusion(f32[5,2,64,256]{3,2,1,0:T(8,128)S(1)} %get-tuple-element.20, f32[32,5,1,1]{0,3,2,1:T(1,128)S(1)} %get-tuple-element.29), kind=kOutput, calls=%fused_computation.50 | convolution fusion | flops 62914560 | bytes 4850304 | tf_op jit(solution)/shard_map/oi,inpw->onpw/dot_general | solution.py:115
  142.0 10.2 %maximum_bitcast_fusion = f32[32,2,64,256]{3,0,2,1:T(8,128)S(1)} fusion(f32[2,64,256,32]{2,3,1,0:T(8,128)} %fusion.38, f32[2,64,256,32]{2,3,1,0:T(8,128)S(1)} %fusion.40, f32[2,64,256,32]{2,3,1,0:T(8,128)} %fusion.42, f32[2,64,256,32]{2,3,1,0:T(8,128)S(1)} %fusion.45, f32[2,64,256,32]{2,3,1,0:T(8,128)} %fusion.47, f32[2,64,256,32]{2,3,1,0:T(8,128)} %fusion.49, ...), kind=kOutput, calls=%fused_computation.24 | convolution fusion | flops 73400320 | bytes 38404864 | tf_op jit(solution)/shard_map/oi,inpw->onpw/dot_general | solution.py:115
  152.2 0.0 copy-start.6
  152.2 3.2 %fusion.114 = (f32[32,2,64,1]{3,0,2,1:T(8,128)}, f32[32,2,64,1]{3,0,2,1:T(8,128)}) fusion(f32[32,2,64,256]{3,0,2,1:T(8,128)S(1)} %maximum_bitcast_fusion), kind=kLoop, calls=%fused_computation.148 | loop fusion | bytes 65536 | tf_op jit(solution)/shard_map/slice | solution.py:28
  155.4 0.1 copy-done.2
  155.5 2.8 %copy.95 = f32[32,2,64,1]{2,0,3,1:T(8,128)S(1)} copy(f32[32,2,64,1]{3,0,2,1:T(8,128)} %get-tuple-element.11) | data formatting | bytes 32768 | tf_op jit(solution)/shard_map/slice | solution.py:28
  158.3 2.3 %collective-permute-start.4 = (f32[32,2,64,1]{2,0,3,1:T(8,128)S(1)}, f32[32,2,64,1]{2,0,3,1:T(8,128)S(1)}, u32[]{:S(2)}, u32[]{:S(2)}) collective-permute-start(f32[32,2,64,1]{2,0,3,1:T(8,128)S(1)} %copy.95), channel_id=1, source_target_pairs={{0,1},{1,2},{2,3},{3,4},{4,5},{5,6},{6,7},{7,8},{8,9},{9,10},{10,1... | collective-permute-start | bytes 49160 | tf_op jit(solution)/shard_map/ppermute | solution.py:30
  160.6 4.5 %fusion.102 = f32[2,64,256,2]{2,3,1,0:T(2,128)S(1)} fusion(f32[32,2,64,256]{3,0,2,1:T(8,128)} %copy-done.2, f32[2,32,3,3]{1,0,3,2:T(2,128)S(1)} %copy-done.6), kind=kOutput, calls=%fused_computation.134 | convolution fusion | flops 25165824 | bytes 4457472 | tf_op jit(solution)/shard_map/oi,inpw->onpw/dot_general | solution.py:115
  165.1 1.1 copy.96
  166.2 6.0 %collective-permute-start.5 = (f32[32,2,64,1]{2,0,3,1:T(8,128)S(1)}, f32[32,2,64,1]{2,0,3,1:T(8,128)S(1)}, u32[]{:S(2)}, u32[]{:S(2)}) collective-permute-start(f32[32,2,64,1]{2,0,3,1:T(8,128)S(1)} %copy.96), channel_id=1, source_target_pairs={{1,0},{2,1},{3,2},{4,3},{5,4},{6,5},{7,6},{8,7},{9,8},{10,9},{11,1... | collective-permute-start | bytes 49160 | tf_op jit(solution)/shard_map/ppermute | solution.py:31
  172.3 1.9 copy.97
  174.1 4.9 %fusion.9 = f32[2,64,256,2]{2,3,1,0:T(2,128)S(1)} fusion(f32[32,2,64,256]{3,0,2,1:T(8,128)} %copy-done.2, f32[32,2,64,1]{3,0,2,1:T(8,128)S(1)} %copy.97, f32[2,32,3,3]{1,0,3,2:T(2,128)S(1)} %copy-done.6), kind=kOutput, calls=%fused_computation.16 | convolution fusion | flops 26214400 | bytes 6554624 | tf_op jit(solution)/shard_map/oi,inpw->onpw/dot_general | solution.py:115
  179.0 2.9 %copy.98 = f32[32,2,64,1]{3,0,2,1:T(8,128)} copy(f32[32,2,64,1]{2,0,3,1:T(8,128)S(1)} %collective-permute-done.5) | data formatting | bytes 32768 | tf_op jit(solution)/shard_map/ppermute | solution.py:31
  181.9 5.0 %select_maximum_fusion = f32[32,2,66,258]{3,0,2,1:T(8,128)S(1)} fusion(f32[32,2,64,1]{3,0,2,1:T(8,128)} %copy.98, f32[32,2,64,256]{3,0,2,1:T(8,128)} %copy-done.2, f32[32,2,64,1]{3,0,2,1:T(8,128)S(1)} %copy.97), kind=kLoop, calls=%fused_computation.3 | loop fusion | flops 8718336 | bytes 8586240 | tf_op jit(solution)/shard_map/concatenate | solution.py:32
  186.9 2.6 %fusion.3 = f32[2,64,256,2]{2,3,1,0:T(2,128)S(1)} fusion(f32[32,2,66,258]{3,0,2,1:T(8,128)S(1)} %select_maximum_fusion, f32[2,32,3,3]{1,0,3,2:T(2,128)S(1)} %copy-done.6), kind=kOutput, calls=%fused_computation.8 | convolution fusion | flops 25165824 | bytes 4457472 | tf_op jit(solution)/shard_map/oi,inpw->onpw/dot_general | solution.py:115
  189.5 2.3 %fusion.5 = f32[2,64,256,2]{2,3,1,0:T(2,128)S(1)} fusion(f32[32,2,66,258]{3,0,2,1:T(8,128)S(1)} %select_maximum_fusion, f32[2,32,3,3]{1,0,3,2:T(2,128)S(1)} %copy-done.6), kind=kOutput, calls=%fused_computation.10 | convolution fusion | flops 25165824 | bytes 4457472 | tf_op jit(solution)/shard_map/oi,inpw->onpw/dot_general | solution.py:115
  191.9 2.6 %fusion.11 = f32[2,64,256,2]{2,3,1,0:T(2,128)S(1)} fusion(f32[32,2,66,258]{3,0,2,1:T(8,128)S(1)} %select_maximum_fusion, f32[2,32,3,3]{1,0,3,2:T(2,128)S(1)} %copy-done.6), kind=kOutput, calls=%fused_computation.18 | convolution fusion | flops 25165824 | bytes 4457472 | tf_op jit(solution)/shard_map/oi,inpw->onpw/dot_general | solution.py:115
  194.5 2.6 %fusion.13 = f32[2,64,256,2]{2,3,1,0:T(2,128)S(1)} fusion(f32[32,2,66,258]{3,0,2,1:T(8,128)S(1)} %select_maximum_fusion, f32[2,32,3,3]{1,0,3,2:T(2,128)S(1)} %copy-done.6), kind=kOutput, calls=%fused_computation.20 | convolution fusion | flops 25165824 | bytes 4457472 | tf_op jit(solution)/shard_map/oi,inpw->onpw/dot_general | solution.py:115
  197.2 2.9 %fusion.1 = f32[2,64,256,2]{2,3,1,0:T(2,128)S(1)} fusion(f32[32,2,66,258]{3,0,2,1:T(8,128)S(1)} %select_maximum_fusion, f32[2,32,3,3]{1,0,3,2:T(2,128)S(1)} %copy-done.6), kind=kOutput, calls=%fused_computation.6 | convolution fusion | flops 25165824 | bytes 4457472 | tf_op jit(solution)/shard_map/oi,inpw->onpw/dot_general | solution.py:115
  200.1 2.4 %fusion.34 = f32[2,64,256,2]{2,3,1,0:T(2,128)S(1)} fusion(f32[2,64,256,2]{2,3,1,0:T(2,128)S(1)} %fusion.102, f32[2,64,256,2]{2,3,1,0:T(2,128)S(1)} %fusion.9, f32[2,64,256,2]{2,3,1,0:T(2,128)S(1)} %fusion.11, f32[2,64,256,2]{2,3,1,0:T(2,128)S(1)} %fusion.13, f32[32,2,66,258]{3,0,2,1:T(8,128)S(1)} %select_maximum_fusion, f32[2]{0:T(128)S(1)} %copy-done.8, ...), kind=kOutput, calls=%fused_computation.37 | convolution fusion | flops 25493504 | bytes 5506560 | tf_op jit(solution)/shard_map/oi,inpw->onpw/dot_general | solution.py:115
  202.5 3.3 %fusion.27 = f32[2,2,64,256]{3,1,2,0:T(2,128)S(1)} fusion(f32[2,64,256,2]{2,3,1,0:T(2,128)S(1)} %fusion.1, f32[2,64,256,2]{2,3,1,0:T(2,128)S(1)} %fusion.3, f32[2,64,256,2]{2,3,1,0:T(2,128)S(1)} %fusion.5, f32[2,64,256,2]{2,3,1,0:T(2,128)S(1)} %fusion.34, f32[32,2,64,1]{3,0,2,1:T(8,128)S(1)} %copy-done.4, f32[32,2,64,256]{3,0,2,1:T(8,128)S(1)} %copy-done.3, ...), kind=kOutput, calls=%fused_computation.34 | convolution fusion | flops 26476544 | bytes 7603200 | tf_op jit(solution)/shard_map/oi,inpw->onpw/dot_general | solution.py:115
  205.8 0.7 copy.101
  (31 shorter events, 0.3 us)
Async XLA Ops:
  6.5 7.2 %copy-start = (s32[32,1,64]{2,1,0:T(1,128)S(1)}, s32[32,1,64]{2,1,0:T(1,128)}, u32[]{:S(2)}) copy-start(s32[32,1,64]{2,1,0:T(1,128)} %param.9) | copy-start | bytes 24580
  6.5 75.3 %copy-start.9 = (s32[64]{0:T(128)S(1)}, s32[64]{0:T(128)}, u32[]{:S(2)}) copy-start(s32[64]{0:T(128)} %param.11) | copy-start | bytes 772
  6.5 16.3 %all-to-all-start = ((bf16[32,2,8,256]{3,2,1,0:T(8,128)(2,1)}), bf16[32,2,8,256]{3,2,1,0:T(8,128)(2,1)S(1)}, u32[]{:S(2)}, u32[]{:S(2)}) async-start(bf16[32,2,8,256]{3,2,1,0:T(8,128)(2,1)} %param.8), calls=%async_computation | async-start | bytes 524288 | tf_op jit(solution)/shard_map/all_to_all | solution.py:146
  13.7 58.7 %all-gather.2.cloned.1.call-start = ((), (), s32[]{:S(2)}) async-start(), calls=%async_computation.1 | async-start | bytes 1114112 | tf_op jit(solution)/shard_map/all_gather | solution.py:13
  73.8 9.0 %collective-permute-start = (bf16[3,2,64,14]{3,2,0,1:T(8,128)(2,1)S(1)}, bf16[3,2,64,14]{3,2,0,1:T(8,128)(2,1)S(1)}, u32[]{:S(2)}, u32[]{:S(2)}) collective-permute-start(bf16[3,2,64,14]{3,2,0,1:T(8,128)(2,1)S(1)} %get-tuple-element.23), channel_id=1, source_target_pairs={{0,1},{1,2},{2,3},{3,4},{4,5},{5,6},{6,7},{7,8},{8,9},{9,10},{10,1... | collective-permute-start | bytes 32264 | tf_op jit(solution)/shard_map/ppermute | solution.py:30
  76.3 8.5 %collective-permute-start.1 = (bf16[3,2,64,14]{3,2,0,1:T(8,128)(2,1)S(1)}, bf16[3,2,64,14]{3,2,0,1:T(8,128)(2,1)S(1)}, u32[]{:S(2)}, u32[]{:S(2)}) collective-permute-start(bf16[3,2,64,14]{3,2,0,1:T(8,128)(2,1)S(1)} %get-tuple-element.24), channel_id=1, source_target_pairs={{1,0},{2,1},{3,2},{4,3},{5,4},{6,5},{7,6},{8,7},{9,8},{10,9},{11,1... | collective-permute-start | bytes 32264 | tf_op jit(solution)/shard_map/ppermute | solution.py:31
  87.1 16.4 %collective-permute-start.2 = (f32[5,2,64,1]{3,2,1,0:T(8,128)S(1)}, f32[5,2,64,1]{3,2,1,0:T(8,128)S(1)}, u32[]{:S(2)}, u32[]{:S(2)}) collective-permute-start(f32[5,2,64,1]{3,2,1,0:T(8,128)S(1)} %get-tuple-element.21), channel_id=1, source_target_pairs={{0,1},{1,2},{2,3},{3,4},{4,5},{5,6},{6,7},{7,8},{8,9},{9,10},{10,1... | collective-permute-start | bytes 7688 | tf_op jit(solution)/shard_map/ppermute | solution.py:30
  89.4 18.1 %collective-permute-start.3 = (f32[5,2,64,1]{3,2,1,0:T(8,128)S(1)}, f32[5,2,64,1]{3,2,1,0:T(8,128)S(1)}, u32[]{:S(2)}, u32[]{:S(2)}) collective-permute-start(f32[5,2,64,1]{3,2,1,0:T(8,128)S(1)} %get-tuple-element.22), channel_id=1, source_target_pairs={{1,0},{2,1},{3,2},{4,3},{5,4},{6,5},{7,6},{8,7},{9,8},{10,9},{11,1... | collective-permute-start | bytes 7688 | tf_op jit(solution)/shard_map/ppermute | solution.py:31
  136.4 5.5 %copy-start.7 = (f32[32]{0:T(128)S(1)}, f32[32]{0:T(128)}, u32[]{:S(2)}) copy-start(f32[32]{0:T(128)} %param.13) | copy-start | bytes 388
  152.2 3.3 %copy-start.2 = (f32[32,2,64,256]{3,0,2,1:T(8,128)}, f32[32,2,64,256]{3,0,2,1:T(8,128)S(1)}, u32[]{:S(2)}) copy-start(f32[32,2,64,256]{3,0,2,1:T(8,128)S(1)} %maximum_bitcast_fusion) | copy-start | bytes 12582916
  152.2 8.4 %copy-start.6 = (f32[2,32,3,3]{1,0,3,2:T(2,128)S(1)}, f32[2,32,3,3]{1,0,3,2:T(2,128)}, u32[]{:S(2)}) copy-start(f32[2,32,3,3]{1,0,3,2:T(2,128)} %param.14) | copy-start | bytes 6916
  155.5 9.6 %copy-start.5 = (f32[32,2,64,1]{3,0,2,1:T(8,128)S(1)}, f32[32,2,64,1]{3,0,2,1:T(8,128)}, u32[]{:S(2)}) copy-start(f32[32,2,64,1]{3,0,2,1:T(8,128)} %get-tuple-element.12) | copy-start | bytes 49156
  158.3 14.0 %collective-permute-start.4 = (f32[32,2,64,1]{2,0,3,1:T(8,128)S(1)}, f32[32,2,64,1]{2,0,3,1:T(8,128)S(1)}, u32[]{:S(2)}, u32[]{:S(2)}) collective-permute-start(f32[32,2,64,1]{2,0,3,1:T(8,128)S(1)} %copy.95), channel_id=1, source_target_pairs={{0,1},{1,2},{2,3},{3,4},{4,5},{5,6},{6,7},{7,8},{8,9},{9,10},{10,1... | collective-permute-start | bytes 49160 | tf_op jit(solution)/shard_map/ppermute | solution.py:30
  166.2 12.8 %collective-permute-start.5 = (f32[32,2,64,1]{2,0,3,1:T(8,128)S(1)}, f32[32,2,64,1]{2,0,3,1:T(8,128)S(1)}, u32[]{:S(2)}, u32[]{:S(2)}) collective-permute-start(f32[32,2,64,1]{2,0,3,1:T(8,128)S(1)} %copy.96), channel_id=1, source_target_pairs={{1,0},{2,1},{3,2},{4,3},{5,4},{6,5},{7,6},{8,7},{9,8},{10,9},{11,1... | collective-permute-start | bytes 49160 | tf_op jit(solution)/shard_map/ppermute | solution.py:31
  194.5 5.5 %copy-start.8 = (f32[2]{0:T(128)S(1)}, f32[2]{0:T(128)}, u32[]{:S(2)}) copy-start(f32[2]{0:T(128)} %param.15) | copy-start | bytes 28
  197.2 5.3 %copy-start.3 = (f32[32,2,64,256]{3,0,2,1:T(8,128)S(1)}, f32[32,2,64,256]{3,0,2,1:T(8,128)}, u32[]{:S(2)}) copy-start(f32[32,2,64,256]{3,0,2,1:T(8,128)} %copy-done.2) | copy-start | bytes 12582916
  197.2 5.3 %copy-start.4 = (f32[32,2,64,1]{3,0,2,1:T(8,128)S(1)}, f32[32,2,64,1]{3,0,2,1:T(8,128)}, u32[]{:S(2)}) copy-start(f32[32,2,64,1]{3,0,2,1:T(8,128)} %copy.98) | copy-start | bytes 49156
  200.1 6.5 %copy-start.1 = (s32[32,1,64]{2,1,0:T(1,128)S(1)}, s32[32,1,64]{2,1,0:T(1,128)}, u32[]{:S(2)}) copy-start(s32[32,1,64]{2,1,0:T(1,128)} %param.9) | copy-start | bytes 24580
Sparse Core Ops, SparseCore 0:
  25.1 47.2 all-gather.1
